TPU v7x, 128 devices: a whole 4x4x4 slice. The times are simulated.
128 devices in a mesh: pipe: 16 (over y_lo, z, core), seq: 8 (over x, y_hi).
Axes of the slice: x: 4, y: 4 (y_hi: 2, y_lo: 2; y = y_hi * 2 + y_lo), z: 4, core: 2. Of those that a mesh axis runs over, the one named last changes fastest.
Arguments:
- x_fwd: float32 [16, 1024, 2048], P('pipe', 'seq'), may hold values from -12 to 12
- x_bwd: float32 [16, 1024, 2048], P('pipe', 'seq'), may hold values from -12 to 12
- grad_in: float32 [16, 1024, 2048], P('pipe', 'seq'), may hold values from -6 to 6
- gain: float32 [16, 2048], P('pipe'), may hold values from 0.25 to 1.75
- w_query: bfloat16 [16, 2048, 2048], P('pipe', None, 'seq'), may hold values from -2 to 2
- w_key: bfloat16 [16, 2048, 2048], P('pipe', None, 'seq'), may hold values from -2 to 2
- w_value: bfloat16 [16, 2048, 2048], P('pipe', None, 'seq'), may hold values from -0.125 to 0.125
- w_out: bfloat16 [16, 2048, 2048], P('pipe', None, 'seq'), may hold values from -0.125 to 0.125
Outputs:
- act_next: float32 [16, 1024, 2048], P('pipe', 'seq')
- grad_prev: float32 [16, 1024, 2048], P('pipe', 'seq')
All inputs are finite; a program needn't handle non-finite values.
Results may differ from a plain program's by a relative error of at most 0.012.
The roundings to bfloat16 on the way count: a program that leaves them out, or rounds other values in their place, can miss the bound.
Values may be sent and summed in bfloat16 or wider, within the bound.
A program may use at most 192 MiB of HBM per device.

v0:
```python
import jax
import jax.numpy as jnp
from jax import lax
from jax.sharding import PartitionSpec as P

HD = 128


def passed_along(value, axis, steps):
    count = lax.axis_size(axis)
    pairs = [(source, (source + steps) % count) for source in range(count)]
    return lax.ppermute(value, axis, pairs)


def rope_tables(positions):
    half_dim = HD // 2
    inverse = 10000.0 ** (-(jnp.arange(half_dim).astype(jnp.float32) * 2.0 / HD))
    angles = positions.astype(jnp.float32)[:, None] * inverse[None, :]
    return (jnp.cos(angles)[:, None, :], jnp.sin(angles)[:, None, :])


def rotate(values, cosine, sine_table):
    shaped = values.reshape(values.shape[0], -1, HD)
    first_half = shaped[..., : HD // 2]
    second_half = shaped[..., HD // 2 :]
    output = jnp.concatenate(
        [
            first_half * cosine - second_half * sine_table,
            second_half * cosine + first_half * sine_table,
        ],
        -1,
    )
    return output.reshape(values.shape)


def rotate_back(values, cosine, sine_table):
    shaped = values.reshape(values.shape[0], -1, HD)
    first_half = shaped[..., : HD // 2]
    second_half = shaped[..., HD // 2 :]
    output = jnp.concatenate(
        [
            first_half * cosine + second_half * sine_table,
            second_half * cosine - first_half * sine_table,
        ],
        -1,
    )
    return output.reshape(values.shape)


def normalize(inputs, gain_row):
    inv_rms = lax.rsqrt(jnp.mean(inputs * inputs, -1, keepdims=True) + 1e-05)
    return ((inputs * inv_rms * gain_row).astype(jnp.bfloat16), inv_rms)


def times_t(left, right):
    return lax.dot_general(
        left, right, (((1,), (1,)), ((), ())), preferred_element_type=jnp.float32
    )


def split_heads(values):
    return values.reshape(values.shape[0], -1, HD)


def attend(query, key_rows, value_rows):
    length = query.shape[0]
    score_scale = HD ** (-0.5)
    key_heads = split_heads(key_rows)
    value_heads = split_heads(value_rows)
    query_blocks = split_heads(query).reshape(length // length, length, -1, HD)

    def one_block(query_block):
        scores = (
            jnp.einsum("qhd,khd->hqk", query_block, key_heads, preferred_element_type=jnp.float32)
            * score_scale
        )
        probs = jax.nn.softmax(scores, axis=-1)
        output = jnp.einsum(
            "hqk,khd->qhd",
            probs.astype(jnp.bfloat16),
            value_heads,
            preferred_element_type=jnp.float32,
        )
        return output.astype(jnp.bfloat16)

    return lax.map(one_block, query_blocks).reshape(length, -1)


def attend_back(query, key_rows, value_rows, grad_out, cosine, sine_table):
    length = query.shape[0]
    score_scale = HD ** (-0.5)
    key_heads = split_heads(key_rows)
    value_heads = split_heads(value_rows)
    query_blocks = split_heads(query).reshape(length // length, length, -1, HD)
    grad_blocks = split_heads(grad_out).reshape(length // length, length, -1, HD)

    def step(totals, operands):
        query_block, grad_block = operands
        scores = (
            jnp.einsum("qhd,khd->hqk", query_block, key_heads, preferred_element_type=jnp.float32)
            * score_scale
        )
        probs = jax.nn.softmax(scores, axis=-1)
        value_grad = jnp.einsum(
            "hqk,qhd->khd",
            probs.astype(jnp.bfloat16),
            grad_block,
            preferred_element_type=jnp.float32,
        )
        prob_grad = jnp.einsum(
            "qhd,khd->hqk", grad_block, value_heads, preferred_element_type=jnp.float32
        )
        row_delta = jnp.sum(probs * prob_grad, -1, keepdims=True)
        score_grad = (probs * (prob_grad - row_delta) * score_scale).astype(jnp.bfloat16)
        query_grad = jnp.einsum(
            "hqk,khd->qhd", score_grad, key_heads, preferred_element_type=jnp.float32
        )
        key_grad = jnp.einsum(
            "hqk,qhd->khd", score_grad, query_block, preferred_element_type=jnp.float32
        )
        return ((totals[0] + key_grad, totals[1] + value_grad), query_grad)

    zero_heads = jnp.zeros(key_heads.shape, jnp.float32)
    (key_total, value_total), query_grads = lax.scan(
        step, (zero_heads, zero_heads), (query_blocks, grad_blocks)
    )
    query_grad = rotate_back(query_grads.reshape(length, -1), cosine, sine_table).astype(
        jnp.bfloat16
    )
    key_grad = rotate_back(key_total.reshape(length, -1), cosine, sine_table).astype(jnp.bfloat16)
    return (query_grad, key_grad, value_total.reshape(length, -1).astype(jnp.bfloat16))


def to_tokens(values):
    return lax.all_to_all(values, "seq", split_axis=1, concat_axis=2, tiled=True)


def shards(x_fwd, x_bwd, grad_in, gain, w_query, w_key, w_value, w_out):
    act_in = x_fwd[0]
    saved_in = x_bwd[0]
    grad = grad_in[0]
    gain_row = gain[0]
    local_rows = act_in.shape[0]
    length = local_rows * lax.axis_size("seq")
    normed_fwd, inv_fwd = normalize(act_in, gain_row)
    normed_bwd, inv_bwd = normalize(saved_in, gain_row)
    grad_low = grad.astype(jnp.bfloat16)
    full_cos, full_sin = rope_tables(jnp.arange(length))
    all_query, all_key, all_value, all_out = (
        lax.all_gather(w_query[0], "seq", axis=1, tiled=True),
        lax.all_gather(w_key[0], "seq", axis=1, tiled=True),
        lax.all_gather(w_value[0], "seq", axis=1, tiled=True),
        lax.all_gather(w_out[0], "seq", axis=1, tiled=True),
    )
    local_cos, local_sin = rope_tables(lax.axis_index("seq") * local_rows + jnp.arange(local_rows))

    def project_local(normed):
        query = rotate(
            jnp.dot(normed, all_query, preferred_element_type=jnp.float32), local_cos, local_sin
        ).astype(jnp.bfloat16)
        key_rows = rotate(
            jnp.dot(normed, all_key, preferred_element_type=jnp.float32), local_cos, local_sin
        ).astype(jnp.bfloat16)
        value_rows = jnp.dot(normed, all_value, preferred_element_type=jnp.float32).astype(
            jnp.bfloat16
        )
        return [query, key_rows, value_rows]

    attn_grad = jnp.dot(grad_low, all_out, preferred_element_type=jnp.float32).astype(jnp.bfloat16)
    pieces = jnp.stack(project_local(normed_fwd) + project_local(normed_bwd) + [attn_grad])
    head_view = lax.all_to_all(pieces, "seq", split_axis=2, concat_axis=1, tiled=True)
    attn = attend(head_view[0], head_view[1], head_view[2])
    attn_tokens = to_tokens(attn[None])[0]
    branch = times_t(attn_tokens, all_out)
    query_grad, key_grad, value_grad = attend_back(
        head_view[3], head_view[4], head_view[5], head_view[6], full_cos, full_sin
    )
    grad_tokens = to_tokens(jnp.stack([query_grad, key_grad, value_grad]))
    d_normed = (
        times_t(grad_tokens[0], all_query)
        + times_t(grad_tokens[1], all_key)
        + times_t(grad_tokens[2], all_value)
    )
    act_out = act_in + branch
    gain_grad = d_normed * gain_row
    d_input = inv_bwd * gain_grad - saved_in * inv_bwd * inv_bwd * inv_bwd * jnp.mean(
        saved_in * gain_grad, -1, keepdims=True
    )
    sent_forward = passed_along(act_out.astype(jnp.bfloat16), "pipe", 1).astype(act_out.dtype)
    sent_backward = passed_along((grad + d_input).astype(jnp.bfloat16), "pipe", -1).astype(
        jnp.float32
    )
    return (sent_forward[None], sent_backward[None])


def solution(mesh):
    placed = (
        P("pipe", "seq", None),
        P("pipe", "seq", None),
        P("pipe", "seq", None),
        P("pipe", None),
        P("pipe", None, "seq"),
        P("pipe", None, "seq"),
        P("pipe", None, "seq"),
        P("pipe", None, "seq"),
    )
    return jax.shard_map(
        shards,
        mesh=mesh,
        in_specs=placed,
        out_specs=(P("pipe", "seq", None), P("pipe", "seq", None)),
        check_vma=False,
    )
```

profile of v0, /device:TPU:1, one launch (start us, length us, event | category | flops | bytes accessed | tf_op | source)
XLA Modules:
  0.0 765.0 jit_solution(12762140533666074192)
XLA Ops:
  13.0 118.5 %all-gather.11.cloned.1.call-done = bf16[1,2048,2048]{2,1,0:T(8,128)(2,1)} async-done(((bf16[1,2048,256]{2,1,0:T(8,128)(2,1)}), bf16[1,2048,2048]{2,1,0:T(8,128)(2,1)}) %all-gather.11.cloned.1.call-update) | async-done | bytes 8388624 | tf_op jit(solution)/shard_map/all_gather | solution.py:151
  131.5 12.4 %copy.67 = bf16[2048,2048]{1,0:T(8,128)(2,1)} copy(bf16[2048,2048]{0,1:T(8,128)(2,1)} %bitcast.212) | data formatting | bytes 16777216 | tf_op jit(solution)/shard_map/dot_general | solution.py:162
  143.8 108.1 %all-gather.9.cloned.1.call-done = bf16[1,2048,2048]{2,1,0:T(8,128)(2,1)} async-done(((bf16[1,2048,256]{2,1,0:T(8,128)(2,1)}), bf16[1,2048,2048]{2,1,0:T(8,128)(2,1)}) %all-gather.9.cloned.1.call-update) | async-done | bytes 8388624 | tf_op jit(solution)/shard_map/all_gather | solution.py:150
  251.9 12.4 %copy.66 = bf16[2048,2048]{1,0:T(8,128)(2,1)} copy(bf16[2048,2048]{0,1:T(8,128)(2,1)} %bitcast.213) | data formatting | bytes 16777216 | tf_op jit(solution)/shard_map/dot_general | solution.py:159
  264.3 6.5 fusion.112
  292.4 80.0 %all-gather.13.cloned.1.call-done = bf16[1,2048,2048]{2,1,0:T(8,128)(2,1)} async-done(((bf16[1,2048,256]{2,1,0:T(8,128)(2,1)}), bf16[1,2048,2048]{2,1,0:T(8,128)(2,1)}) %all-gather.13.cloned.1.call-update) | async-done | bytes 8388624 | tf_op jit(solution)/shard_map/all_gather | solution.py:152
  372.5 5.6 fusion.76
  382.4 110.4 %all-gather.15.cloned.1.call-done = bf16[1,2048,2048]{2,1,0:T(8,128)(2,1)} async-done(((bf16[1,2048,256]{2,1,0:T(8,128)(2,1)}), bf16[1,2048,2048]{2,1,0:T(8,128)(2,1)}) %all-gather.15.cloned.1.call-update) | async-done | bytes 8388624 | tf_op jit(solution)/shard_map/all_gather | solution.py:153
  498.3 6.5 copy.72
  511.1 56.6 %all-to-all-done = bf16[7,128,2048]{1,0,2:T(8,128)(2,1)} async-done(((bf16[7,128,2048]{1,0,2:T(8,128)(2,1)}), bf16[7,128,2048]{1,0,2:T(8,128)(2,1)}, u32[]{:S(2)}, u32[]{:S(2)}) %all-to-all-start) | async-done | bytes 3670048 | tf_op jit(solution)/shard_map/all_to_all | solution.py:171
  582.7 5.7 fusion.127
  588.4 7.2 fusion.124
  595.6 5.9 fusion.86
  601.5 14.8 %fusion.82 = f32[1024,2,128]{0,2,1:T(8,128)} fusion(bf16[1024,2,128]{0,2,1:T(8,128)(2,1)} %squeeze.55, f32[2,1024,1024]{1,2,0:T(8,128)} %fusion.127, f32[2,1024,1024]{1,2,0:T(8,128)} %get-tuple-element.78, f32[2,1024]{1,0:T(2,128)S(1)} %get-tuple-element.77), kind=kOutput, calls=%fused_computation.52 | convolution fusion | flops 551554048 | bytes 18358272 | tf_op jit(solution)/shard_map/while/body/eval_jaxpr/hqk,qhd->khd/dot_general | solution.py:118
  616.2 14.8 %fusion.79 = f32[1024,2,128]{0,2,1:T(8,128)} fusion(bf16[1024,2,128]{0,2,1:T(8,128)(2,1)} %reshape_squeeze.14, f32[2,1024,1024]{1,2,0:T(8,128)} %fusion.127, f32[2,1024,1024]{1,2,0:T(8,128)} %get-tuple-element.78, f32[2,1024]{1,0:T(2,128)S(1)} %get-tuple-element.77), kind=kOutput, calls=%fused_computation.51 | convolution fusion | flops 551554048 | bytes 18358272 | tf_op jit(solution)/shard_map/while/body/eval_jaxpr/hqk,khd->qhd/dot_general | solution.py:115
  637.3 7.2 fusion.123
  653.7 5.6 reduce
  681.8 6.0 pad_maximum_fusion
  687.7 6.6 all-to-all-start.2
  702.0 7.3 fusion.58
  713.3 9.9 %all-to-all-done.2 = bf16[3,1024,256]{2,0,1:T(4,128)(2,1)} async-done(((bf16[3,1024,256]{2,0,1:T(4,128)(2,1)}), bf16[3,1024,256]{2,0,1:T(4,128)(2,1)}, u32[]{:S(2)}, u32[]{:S(2)}) %all-to-all-start.2) | async-done | bytes 1572896 | tf_op jit(solution)/shard_map/all_to_all | solution.py:135
  730.0 6.6 fusion.13
  736.6 6.5 fusion.37
  751.0 5.9 collective-permute-done.1
  (97 shorter events, 123.7 us)
Async XLA Ops:
  7.2 124.3 %all-gather.11.cloned.1.call-start = ((), (), s32[]{:S(2)}) async-start(), calls=%async_computation.4 | async-start | bytes 9437184 | tf_op jit(solution)/shard_map/all_gather | solution.py:151
  7.9 244.0 %all-gather.9.cloned.1.call-start = ((), (), s32[]{:S(2)}) async-start(), calls=%async_computation.3 | async-start | bytes 9437184 | tf_op jit(solution)/shard_map/all_gather | solution.py:150
  8.6 363.8 %all-gather.13.cloned.1.call-start = ((), (), s32[]{:S(2)}) async-start(), calls=%async_computation.5 | async-start | bytes 9437184 | tf_op jit(solution)/shard_map/all_gather | solution.py:152
  9.4 483.4 %all-gather.15.cloned.1.call-start = ((), (), s32[]{:S(2)}) async-start(), calls=%async_computation.6 | async-start | bytes 9437184 | tf_op jit(solution)/shard_map/all_gather | solution.py:153
  251.9 12.4 %copy-start.2 = (f32[1,128,2048]{2,1,0:T(8,128)S(1)}, f32[1,128,2048]{2,1,0:T(8,128)}, u32[]{:S(2)}) copy-start(f32[1,128,2048]{2,1,0:T(8,128)} %param.9) | copy-start | bytes 3145732
  251.9 12.4 %copy-start.7 = (f32[1,2048]{1,0:T(1,128)S(1)}, f32[1,2048]{1,0:T(1,128)}, u32[]{:S(2)}) copy-start(f32[1,2048]{1,0:T(1,128)} %param.11) | copy-start | bytes 24580
  264.3 6.5 copy-start.1
  264.3 6.6 copy-start.3
  264.3 9.1 %slice-start.2 = ((s8[8388608]{0:T(1024)(128)(4,1)}), s8[4194304]{0:T(1024)(128)(4,1)S(1)}, s32[]{:S(2)}) async-start(s8[8388608]{0:T(1024)(128)(4,1)} %bitcast.208), calls=%async_computation.9 | async-start | bytes 8388608
  270.9 2.7 slice-start.3
  372.5 7.3 copy-start
  379.8 113.0 %copy-start.4 = (f32[1,128,2048]{2,1,0:T(8,128)S(1)}, f32[1,128,2048]{2,1,0:T(8,128)}, u32[]{:S(2)}) copy-start(f32[1,128,2048]{2,1,0:T(8,128)} %param.10) | copy-start | bytes 3145732
  504.7 62.9 %all-to-all-start = ((bf16[7,128,2048]{1,0,2:T(8,128)(2,1)}), bf16[7,128,2048]{1,0,2:T(8,128)(2,1)}, u32[]{:S(2)}, u32[]{:S(2)}) async-start(bf16[7,128,2048]{1,0,2:T(8,128)(2,1)} %copy.72), calls=%async_computation | async-start | bytes 8388608 | tf_op jit(solution)/shard_map/all_to_all | solution.py:171
  661.3 26.4 %all-to-all-start.1 = ((bf16[8,2,16384]{2,1,0:T(2,128)(2,1)}), bf16[8,2,16384]{2,1,0:T(2,128)(2,1)}, u32[]{:S(2)}, u32[]{:S(2)}) async-start(bf16[8,2,16384]{2,1,0:T(2,128)(2,1)} %reshape.321), calls=%async_computation.1 | async-start | bytes 1048576 | tf_op jit(solution)/shard_map/all_to_all | solution.py:135
  687.7 35.4 %all-to-all-start.2 = ((bf16[3,1024,256]{2,0,1:T(4,128)(2,1)}), bf16[3,1024,256]{2,0,1:T(4,128)(2,1)}, u32[]{:S(2)}, u32[]{:S(2)}) async-start(bf16[3,1024,256]{2,0,1:T(4,128)(2,1)} %pad_maximum_fusion), calls=%async_computation.2 | async-start | bytes 4194304 | tf_op jit(solution)/shard_map/all_to_all | solution.py:135
  709.2 39.6 %collective-permute-start = (bf16[128,2048]{1,0:T(8,128)(2,1)}, bf16[128,2048]{1,0:T(8,128)(2,1)}, u32[]{:S(2)}, u32[]{:S(2)}) collective-permute-start(bf16[128,2048]{1,0:T(8,128)(2,1)} %fusion.58), channel_id=1, source_target_pairs={{0,8},{8,16},{16,24},{24,32},{32,40},{40,48},{48,56},{56,64},{64,7... | collective-permute-start | bytes 1572872 | tf_op jit(solution)/shard_map/ppermute | solution.py:12
  729.9 6.6 copy-start.6
  729.9 13.1 %slice-start = ((s8[8388608]{0:T(1024)(128)(4,1)}), s8[4194304]{0:T(1024)(128)(4,1)S(1)}, s32[]{:S(2)}) async-start(s8[8388608]{0:T(1024)(128)(4,1)} %bitcast.204), calls=%async_computation.7 | async-start | bytes 8388608
  730.0 13.1 %copy-start.5 = (bf16[1,128,8,256]{1,3,2,0:T(8,128)(2,1)S(1)}, bf16[1,128,8,256]{1,3,2,0:T(8,128)(2,1)}, u32[]{:S(2)}) copy-start(bf16[1,128,8,256]{1,3,2,0:T(8,128)(2,1)} %copy.92) | copy-start | bytes 1572868
  736.6 6.5 slice-start.1
  746.4 10.5 %collective-permute-start.1 = (bf16[128,2048]{1,0:T(8,128)(2,1)S(1)}, bf16[128,2048]{1,0:T(8,128)(2,1)S(1)}, u32[]{:S(2)}, u32[]{:S(2)}) collective-permute-start(bf16[128,2048]{1,0:T(8,128)(2,1)S(1)} %fusion.89), channel_id=1, source_target_pairs={{0,120},{8,0},{16,8},{24,16},{32,24},{40,32},{48,40},{56,48},{64,5... | collective-permute-start | bytes 1572872 | tf_op jit(solution)/shard_map/ppermute | solution.py:12
Sparse Core Ops, SparseCore 0:
  10.2 121.2 all-gather.10
  133.6 118.2 all-gather.8
  254.1 118.3 all-gather.12
  374.5 118.2 all-gather.14
where the time goes:
time: 777 us; the launch traced here: 765 us
  waiting for transfers between devices  492 us (63%)
  matrix products  112 us (14%)
  local copies, waits for them, and re-layouts  95 us (12%)
  other arithmetic  29.8 us (4%)
  starting transfers between devices  22.1 us (3%)
  between operations  14.4 us (2%)
    all_gather x1, waiting for transfers between devices, shards(): lax.all_gather(w_key[0], 'seq', axis=1, tiled=True)  118 us
    all_gather x1, waiting for transfers between devices, shards(): lax.all_gather(w_out[0], 'seq', axis=1, tiled=True)  110 us
    all_gather x1, waiting for transfers between devices, shards(): lax.all_gather(w_query[0], 'seq', axis=1, tiled=True)  108 us
    all_gather x1, waiting for transfers between devices, shards(): lax.all_gather(w_value[0], 'seq', axis=1, tiled=True)  80 us
    all_to_all x1, waiting for transfers between devices, shards(): lax.all_to_all(pieces, 'seq', split_axis=2, concat_axis=1, tiled=True)  56.6 us
    dot_general x4, matrix products, times_t(): lax.dot_general(left, right, (((1,), (1,)), ((), ())), preferred_element_...  23.4 us
  transfers between devices with their start and end apart: 9, of which 7 were waited for; matrix products, arithmetic and copies ran while one was open for 17% of the time, Pallas kernels for 0%

commit v1 on v0

--- a/solution.py
+++ b/solution.py
@@ -149,7 +149,7 @@
     all_query, all_key, all_value, all_out = (
         lax.all_gather(w_query[0], "seq", axis=1, tiled=True),
         lax.all_gather(w_key[0], "seq", axis=1, tiled=True),
-        lax.all_gather(w_value[0], "seq", axis=1, tiled=True),
+        jnp.concatenate(lax.all_gather(w_value[0], "seq"), 1),
         lax.all_gather(w_out[0], "seq", axis=1, tiled=True),
     )
     local_cos, local_sin = rope_tables(lax.axis_index("seq") * local_rows + jnp.arange(local_rows))

time: 777 us -> 730 us (0.940)
  waiting for transfers between devices: 492 us -> 470 us
  local copies, waits for them, and re-layouts: 95 us -> 79 us
    all_gather x1, waiting for transfers between devices: 110 us -> 91.9 us  [shards(): lax.all_gather(w_out[0], 'seq', axis=1, tiled=True)]
    all_gather x0 -> x1, local copies, waits for them, and re-layouts: none -> 11.8 us  [shards(): lax.all_gather(w_value[0], 'seq')]
  transfers between devices with their start and end apart: 9 -> 9, of which waited for: 7 -> 7; matrix products, arithmetic and copies ran while one was open for 17% -> 18% of each run, Pallas kernels for 0% -> 0%
where the time goes in v1:
time: 730 us; the launch traced here: 719 us
  waiting for transfers between devices  470 us (64%)
  matrix products  106 us (15%)
  local copies, waits for them, and re-layouts  79 us (11%)
  other arithmetic  28.4 us (4%)
  starting transfers between devices  22.1 us (3%)
  between operations  14.6 us (2%)
    all_gather x1, waiting for transfers between devices, shards(): lax.all_gather(w_key[0], 'seq', axis=1, tiled=True)  117 us
    all_gather x1, waiting for transfers between devices, shards(): lax.all_gather(w_query[0], 'seq', axis=1, tiled=True)  109 us
    all_gather x1, waiting for transfers between devices, shards(): lax.all_gather(w_out[0], 'seq', axis=1, tiled=True)  91.9 us
    all_gather x1, waiting for transfers between devices, shards(): lax.all_gather(w_value[0], 'seq')  77.5 us
    all_to_all x1, waiting for transfers between devices, shards(): lax.all_to_all(pieces, 'seq', split_axis=2, concat_axis=1, tiled=True)  56.6 us
    dot_general x4, matrix products, times_t(): lax.dot_general(left, right, (((1,), (1,)), ((), ())), preferred_element_...  21.6 us
    dot_general x1, matrix products, step(): jnp.einsum('hqk,qhd->khd', score_grad, query_block, preferred_element_typ...  14.7 us
  transfers between devices with their start and end apart: 9, of which 7 were waited for; matrix products, arithmetic and copies ran while one was open for 18% of the time, Pallas kernels for 0%

profile of v1, /device:TPU:1, one launch (start us, length us, event | category | flops | bytes accessed | tf_op | source)
XLA Modules:
  0.0 719.4 jit_solution(18219292756745799930)
XLA Ops:
  14.8 116.7 %all-gather.12.cloned.1.call-done = bf16[1,2048,2048]{2,1,0:T(8,128)(2,1)} async-done(((bf16[1,2048,256]{2,1,0:T(8,128)(2,1)}), bf16[1,2048,2048]{2,1,0:T(8,128)(2,1)}) %all-gather.12.cloned.1.call-update) | async-done | bytes 8388624 | tf_op jit(solution)/shard_map/all_gather | solution.py:151
  131.5 11.9 %copy.69 = bf16[2048,2048]{1,0:T(8,128)(2,1)} copy(bf16[2048,2048]{0,1:T(8,128)(2,1)} %bitcast.201) | data formatting | bytes 16777216 | tf_op jit(solution)/shard_map/dot_general | solution.py:162
  143.3 108.6 %all-gather.10.cloned.1.call-done = bf16[1,2048,2048]{2,1,0:T(8,128)(2,1)} async-done(((bf16[1,2048,256]{2,1,0:T(8,128)(2,1)}), bf16[1,2048,2048]{2,1,0:T(8,128)(2,1)}) %all-gather.10.cloned.1.call-update) | async-done | bytes 8388624 | tf_op jit(solution)/shard_map/all_gather | solution.py:150
  251.9 12.3 %copy.68 = bf16[2048,2048]{1,0:T(8,128)(2,1)} copy(bf16[2048,2048]{0,1:T(8,128)(2,1)} %bitcast.202) | data formatting | bytes 16777216 | tf_op jit(solution)/shard_map/dot_general | solution.py:159
  264.2 6.6 fusion.76
  284.6 77.5 %all-gather.8.cloned.1.call-done = bf16[8,2048,256]{2,1,0:T(8,128)(2,1)} async-done(((bf16[1,2048,256]{2,1,0:T(8,128)(2,1)}), bf16[8,2048,256]{2,1,0:T(8,128)(2,1)}) %all-gather.8.cloned.1.call-update) | async-done | bytes 8388624 | tf_op jit(solution)/shard_map/all_gather | solution.py:152
  362.1 11.8 %copy.70 = bf16[8,2048,256]{1,2,0:T(8,128)(2,1)} copy(bf16[8,2048,256]{2,1,0:T(8,128)(2,1)} %all-gather.8.cloned.1.call-done) | data formatting | bytes 16777216 | tf_op jit(solution)/shard_map/all_gather | solution.py:152
  375.6 7.9 %fusion.45 = bf16[7,128,2048]{2,1,0:T(8,128)(2,1)} fusion(bf16[7,128,2048]{2,1,0:T(8,128)(2,1)} %constant_dynamic-update-slice_fusion.2, bf16[2048,2048]{0,1:T(8,128)(2,1)} %bitcast.190, bf16[1,128,2048]{2,1,0:T(8,128)(2,1)S(1)} %get-tuple-element.72), kind=kOutput, calls=%fused_computation.39 | convolution fusion | flops 1074003968 | bytes 9437184 | tf_op jit(solution)/shard_map/dot_general | solution.py:164
  389.0 91.9 %all-gather.14.cloned.1.call-done = bf16[1,2048,2048]{2,1,0:T(8,128)(2,1)} async-done(((bf16[1,2048,256]{2,1,0:T(8,128)(2,1)}), bf16[1,2048,2048]{2,1,0:T(8,128)(2,1)}) %all-gather.14.cloned.1.call-update) | async-done | bytes 8388624 | tf_op jit(solution)/shard_map/all_gather | solution.py:153
  480.9 5.4 fusion.51
  486.3 6.5 copy.75
  499.1 56.6 %all-to-all-done = bf16[7,128,2048]{1,0,2:T(8,128)(2,1)} async-done(((bf16[7,128,2048]{1,0,2:T(8,128)(2,1)}), bf16[7,128,2048]{1,0,2:T(8,128)(2,1)}, u32[]{:S(2)}, u32[]{:S(2)}) %all-to-all-start) | async-done | bytes 3670048 | tf_op jit(solution)/shard_map/all_to_all | solution.py:171
  565.9 7.2 %fusion.96 = (f32[2,1024]{1,0:T(2,128)S(1)}, f32[2,1024,1024]{1,2,0:T(8,128)}) fusion(bf16[1024,2,128]{0,2,1:T(8,128)(2,1)} %squeeze.51, bf16[1024,2,128]{0,2,1:T(8,128)(2,1)} %reshape_squeeze.14), kind=kOutput, calls=%fused_computation.120 | convolution fusion | flops 543163392 | bytes 9445376 | tf_op jit(solution)/shard_map/while/body/eval_jaxpr/sub | solution.py:103
  573.2 5.4 fusion.99
  581.5 12.5 %fusion.54 = f32[1024,2,128]{0,2,1:T(8,128)S(1)} fusion(bf16[1024,2,128]{0,2,1:T(8,128)(2,1)} %reshape_squeeze.14, f32[2,1024,1024]{1,2,0:T(8,128)} %fusion.99, f32[2,1024,1024]{1,2,0:T(8,128)} %get-tuple-element.80, f32[2,1024]{1,0:T(2,128)S(1)} %get-tuple-element.79), kind=kOutput, calls=%fused_computation.45 | convolution fusion | flops 551554048 | bytes 18358272 | tf_op jit(solution)/shard_map/while/body/eval_jaxpr/hqk,khd->qhd/dot_general | solution.py:115
  594.1 14.7 %fusion.57 = f32[1024,2,128]{0,2,1:T(8,128)} fusion(bf16[1024,2,128]{0,2,1:T(8,128)(2,1)} %squeeze.51, f32[2,1024,1024]{1,2,0:T(8,128)} %fusion.99, f32[2,1024,1024]{1,2,0:T(8,128)} %get-tuple-element.80, f32[2,1024]{1,0:T(2,128)S(1)} %get-tuple-element.79), kind=kOutput, calls=%fused_computation.46 | convolution fusion | flops 551554048 | bytes 18358272 | tf_op jit(solution)/shard_map/while/body/eval_jaxpr/hqk,qhd->khd/dot_general | solution.py:118
  611.1 7.1 fusion.95
  644.0 5.6 pad_maximum_fusion
  649.7 6.6 all-to-all-start.2
  663.9 7.3 %fusion.41 = bf16[128,2048]{1,0:T(8,128)(2,1)} fusion(bf16[128,2048]{0,1:T(8,128)(2,1)} %bitcast.211, bf16[1,2048,2048]{2,1,0:T(8,128)(2,1)} %all-gather.14.cloned.1.call-done, f32[1,128,2048]{2,1,0:T(8,128)S(1)} %copy-done.3), kind=kOutput, calls=%fused_computation.37 | convolution fusion | flops 1074266112 | bytes 10485760 | tf_op jit(solution)/shard_map/dot_general | solution.py:56
  675.2 9.9 %all-to-all-done.2 = bf16[3,1024,256]{2,0,1:T(4,128)(2,1)S(1)} async-done(((bf16[3,1024,256]{2,0,1:T(4,128)(2,1)}), bf16[3,1024,256]{2,0,1:T(4,128)(2,1)S(1)}, u32[]{:S(2)}, u32[]{:S(2)}) %all-to-all-start.2) | async-done | bytes 1572896 | tf_op jit(solution)/shard_map/all_to_all | solution.py:135
  686.3 6.5 fusion.7
  692.7 6.5 fusion.31
  705.5 5.9 collective-permute-done.1
  (106 shorter events, 96.0 us)
Async XLA Ops:
  7.2 124.3 %all-gather.12.cloned.1.call-start = ((), (), s32[]{:S(2)}) async-start(), calls=%async_computation.5 | async-start | bytes 9437184 | tf_op jit(solution)/shard_map/all_gather | solution.py:151
  7.9 244.0 %all-gather.10.cloned.1.call-start = ((), (), s32[]{:S(2)}) async-start(), calls=%async_computation.4 | async-start | bytes 9437184 | tf_op jit(solution)/shard_map/all_gather | solution.py:150
  8.6 353.5 %all-gather.8.cloned.1.call-start = ((), (), s32[]{:S(2)}) async-start(), calls=%async_computation.3 | async-start | bytes 9437184 | tf_op jit(solution)/shard_map/all_gather | solution.py:152
  9.4 471.5 %all-gather.14.cloned.1.call-start = ((), (), s32[]{:S(2)}) async-start(), calls=%async_computation.6 | async-start | bytes 9437184 | tf_op jit(solution)/shard_map/all_gather | solution.py:153
  264.2 6.6 copy-start.1
  264.2 9.0 %slice-start.2 = ((s8[8388608]{0:T(1024)(128)(4,1)}), s8[4194304]{0:T(1024)(128)(4,1)S(1)}, s32[]{:S(2)}) async-start(s8[8388608]{0:T(1024)(128)(4,1)} %bitcast.197), calls=%async_computation.9 | async-start | bytes 8388608
  270.8 2.6 slice-start.3
  373.9 11.4 %copy-start = (bf16[8,2048,256]{1,2,0:T(8,128)(2,1)S(1)}, bf16[8,2048,256]{1,2,0:T(8,128)(2,1)}, u32[]{:S(2)}) copy-start(bf16[8,2048,256]{1,2,0:T(8,128)(2,1)} %copy.70) | copy-start | bytes 25165828
  375.6 105.2 %copy-start.4 = (f32[1,128,2048]{2,1,0:T(8,128)S(1)}, f32[1,128,2048]{2,1,0:T(8,128)}, u32[]{:S(2)}) copy-start(f32[1,128,2048]{2,1,0:T(8,128)} %param.10) | copy-start | bytes 3145732
  492.8 62.9 %all-to-all-start = ((bf16[7,128,2048]{1,0,2:T(8,128)(2,1)}), bf16[7,128,2048]{1,0,2:T(8,128)(2,1)}, u32[]{:S(2)}, u32[]{:S(2)}) async-start(bf16[7,128,2048]{1,0,2:T(8,128)(2,1)} %copy.75), calls=%async_computation | async-start | bytes 8388608 | tf_op jit(solution)/shard_map/all_to_all | solution.py:171
  564.7 8.5 %copy-start.6 = (bf16[1024,2,128]{0,2,1:T(8,128)(2,1)S(1)}, bf16[1024,2,128]{0,2,1:T(8,128)(2,1)}, u32[]{:S(2)}) copy-start(bf16[1024,2,128]{0,2,1:T(8,128)(2,1)} %squeeze.52) | copy-start | bytes 1572868
  573.2 6.1 copy-start.10
  610.0 8.1 %copy-start.8 = (bf16[1024,2,128]{0,2,1:T(8,128)(2,1)S(1)}, bf16[1024,2,128]{0,2,1:T(8,128)(2,1)}, u32[]{:S(2)}) copy-start(bf16[1024,2,128]{0,2,1:T(8,128)(2,1)} %reshape_squeeze.12) | copy-start | bytes 1572868
  618.1 14.7 %copy-start.7 = (f32[1024,64]{0,1:T(8,128)S(1)}, f32[1024,64]{0,1:T(8,128)}, u32[]{:S(2)}) copy-start(f32[1024,64]{0,1:T(8,128)} %get-tuple-element.74) | copy-start | bytes 786436
  628.4 21.2 %all-to-all-start.1 = ((bf16[8,2,16384]{2,1,0:T(2,128)(2,1)}), bf16[8,2,16384]{2,1,0:T(2,128)(2,1)}, u32[]{:S(2)}, u32[]{:S(2)}) async-start(bf16[8,2,16384]{2,1,0:T(2,128)(2,1)} %reshape.356), calls=%async_computation.1 | async-start | bytes 1048576 | tf_op jit(solution)/shard_map/all_to_all | solution.py:135
  638.5 25.4 %copy-start.3 = (f32[1,128,2048]{2,1,0:T(8,128)S(1)}, f32[1,128,2048]{2,1,0:T(8,128)}, u32[]{:S(2)}) copy-start(f32[1,128,2048]{2,1,0:T(8,128)} %param.8) | copy-start | bytes 3145732
  649.7 35.4 %all-to-all-start.2 = ((bf16[3,1024,256]{2,0,1:T(4,128)(2,1)}), bf16[3,1024,256]{2,0,1:T(4,128)(2,1)S(1)}, u32[]{:S(2)}, u32[]{:S(2)}) async-start(bf16[3,1024,256]{2,0,1:T(4,128)(2,1)} %pad_maximum_fusion), calls=%async_computation.2 | async-start | bytes 4194304 | tf_op jit(solution)/shard_map/all_to_all | solution.py:135
  671.2 32.2 %collective-permute-start = (bf16[128,2048]{1,0:T(8,128)(2,1)}, bf16[128,2048]{1,0:T(8,128)(2,1)}, u32[]{:S(2)}, u32[]{:S(2)}) collective-permute-start(bf16[128,2048]{1,0:T(8,128)(2,1)} %fusion.41), channel_id=1, source_target_pairs={{0,8},{8,16},{16,24},{24,32},{32,40},{40,48},{48,56},{56,64},{64,7... | collective-permute-start | bytes 1572872 | tf_op jit(solution)/shard_map/ppermute | solution.py:12
  686.2 13.0 %slice-start = ((s8[8388608]{0:T(1024)(128)(4,1)}), s8[4194304]{0:T(1024)(128)(4,1)S(1)}, s32[]{:S(2)}) async-start(s8[8388608]{0:T(1024)(128)(4,1)} %bitcast.192), calls=%async_computation.7 | async-start | bytes 8388608
  686.2 13.0 %copy-start.2 = (f32[1,128,2048]{2,1,0:T(8,128)S(1)}, f32[1,128,2048]{2,1,0:T(8,128)}, u32[]{:S(2)}) copy-start(f32[1,128,2048]{2,1,0:T(8,128)} %param.9) | copy-start | bytes 3145732
  686.3 13.0 %copy-start.9 = (f32[1,2048]{1,0:T(1,128)S(1)}, f32[1,2048]{1,0:T(1,128)}, u32[]{:S(2)}) copy-start(f32[1,2048]{1,0:T(1,128)} %param.11) | copy-start | bytes 24580
  692.7 6.5 slice-start.1
  699.3 1.4 copy-start.5
  701.0 10.4 %collective-permute-start.1 = (bf16[128,2048]{1,0:T(8,128)(2,1)S(1)}, bf16[128,2048]{1,0:T(8,128)(2,1)S(1)}, u32[]{:S(2)}, u32[]{:S(2)}) collective-permute-start(bf16[128,2048]{1,0:T(8,128)(2,1)S(1)} %fusion.64), channel_id=1, source_target_pairs={{0,120},{8,0},{16,8},{24,16},{32,24},{40,32},{48,40},{56,48},{64,5... | collective-permute-start | bytes 1572872 | tf_op jit(solution)/shard_map/ppermute | solution.py:12
Sparse Core Ops, SparseCore 0:
  10.2 121.2 all-gather.11
  133.6 118.2 all-gather.9
  254.3 107.7 all-gather.7
  364.1 116.6 all-gather.13
